TPU v7x, 256 devices: a whole 4x4x8 slice. The times are simulated.
256 devices in a mesh: dp: 32 (over y, z), head: 4 (over x), rep: 2 (over core).
Axes of the slice: x: 4, y: 4, z: 8, core: 2. Of those that a mesh axis runs over, the one named last changes fastest.
Arguments:
- embeddings: bfloat16 [16384, 8, 1152], P(('dp', 'head', 'rep')), may hold values from -6 to 6
- coverage: int32 [16384, 2], P(('dp', 'head', 'rep')), may hold values from 0 to 127, all different within a row; in each aligned block of 64 rows (0 to 63, 64 to 127, ...) at most 2 rows name the same one
- labels: int32 [16384, 2, 8], P(('dp', 'head', 'rep')), may hold values 0 or 1
- w_in: bfloat16 [128, 1152, 768], P(('dp', 'head')), may hold values from -0.1875 to 0.1875
- bias_in: bfloat16 [128, 768], P(('dp', 'head')), may hold values from -3 to 3
- w_out: bfloat16 [128, 768], P(('dp', 'head')), may hold values from -0.21875 to 0.21875
- first_w: float32 [128, 1152, 768], P(('dp', 'head'), 'rep'), may hold values from -0.5 to 0.5
- second_w: float32 [128, 1152, 768], P(('dp', 'head'), 'rep'), may hold values from 0.0001 to 0.001
- first_vec: float32 [128, 2, 768], P(('dp', 'head')), may hold values from -0.5 to 0.5
- second_vec: float32 [128, 2, 768], P(('dp', 'head')), may hold values from 0.0001 to 0.01
Outputs:
- new_w_in: bfloat16 [128, 1152, 768], P(('dp', 'head'))
- new_vec: bfloat16 [128, 2, 768], P(('dp', 'head'))
- new_first_w: float32 [128, 1152, 768], P(('dp', 'head'), 'rep')
- new_second_w: float32 [128, 1152, 768], P(('dp', 'head'), 'rep')
- new_first_vec: float32 [128, 2, 768], P(('dp', 'head'))
- new_second_vec: float32 [128, 2, 768], P(('dp', 'head'))
Inputs may be any that keep to these rules, and one draw needn't show every extreme that they name: `coverage`: each block names 2 different heads. Among the 64 blocks of one device (aligned blocks of rows, in order) no head is named more than 2 times, a bound that some block reaches; every head is named by some block.
All inputs are finite; a program needn't handle non-finite values. No bound on the sum of `labels` on one device may be relied on, other than what follows from the above.
Results may differ from a plain program's by a relative error of at most 0.00155.
Values may be sent and summed in bfloat16 or wider, within the bound.
A program may use at most 128 MiB of HBM per device.

v0:
```python
import jax
import jax.numpy as jnp
from jax import lax
from jax.sharding import PartitionSpec as P

beta_one = 0.9
beta_two = 0.999
learn_rate = 0.001
epsilon = 1e-08


def per_device(
    embeddings, coverage, labels, w_in, bias_in, w_out, first_w, second_w, first_vec, second_vec
):
    dp_count = lax.axis_size("dp")
    head_count = lax.axis_size("head")
    owners = dp_count * head_count
    block_count, rows_block, feature = embeddings.shape
    per_block = coverage.shape[1]
    slot_count = 2 * block_count * per_block // owners
    entries = block_count * per_block
    heads_flat = coverage.reshape(entries)
    onehot = (heads_flat[:, None] == jnp.arange(owners, dtype=jnp.int32)[None, :]).astype(jnp.int32)
    slot_rank = jnp.sum((jnp.cumsum(onehot, axis=0) - 1) * onehot, axis=1)
    target_slot = heads_flat * slot_count + slot_rank
    picker = jnp.arange(owners * slot_count, dtype=jnp.int32)[:, None] == target_slot[None, :]
    block_pick = jnp.sum(
        picker.reshape(owners * slot_count, block_count, per_block).astype(jnp.int32), axis=2
    ).astype(jnp.bfloat16)
    send_rows = jnp.dot(
        block_pick,
        embeddings.reshape(block_count, rows_block * feature),
        preferred_element_type=jnp.float32,
    ).astype(jnp.bfloat16)
    label_marks = (labels.reshape(entries, rows_block) + 1).astype(jnp.float32)
    send_marks = jnp.dot(
        picker.astype(jnp.float32), label_marks, precision=lax.Precision.HIGHEST
    ).astype(jnp.bfloat16)
    direct_rows = send_rows.reshape(owners, slot_count, rows_block, feature)
    direct_marks = send_marks.reshape(owners, slot_count, rows_block)
    got_rows, got_marks = (
        lax.all_to_all(direct_rows, ("dp", "head"), split_axis=0, concat_axis=0, tiled=True),
        lax.all_to_all(direct_marks, ("dp", "head"), split_axis=0, concat_axis=0, tiled=True),
    )
    row_data = got_rows.reshape(-1, feature)
    marks_all = got_marks.reshape(-1).astype(jnp.float32)
    usable = marks_all > 0.5
    target = marks_all - 1.0
    out_weight = w_out[0].astype(jnp.float32)
    pre_act = (
        jnp.dot(row_data, w_in[0], preferred_element_type=jnp.float32)
        + bias_in[0].astype(jnp.float32)[None, :]
    )
    sig_pre = jax.nn.sigmoid(pre_act)
    hidden = pre_act * sig_pre
    logits = jnp.sum(hidden * out_weight[None, :], axis=1)
    residual = jnp.where(usable, jax.nn.sigmoid(logits) - target, jnp.zeros_like(logits))
    grad_pre = residual[:, None] * out_weight[None, :] * sig_pre * (1.0 + pre_act * (1.0 - sig_pre))
    grad_low = grad_pre.astype(jnp.bfloat16)
    vec_part = jnp.stack([jnp.sum(grad_pre, axis=0), jnp.sum(residual[:, None] * hidden, axis=0)])
    half_rows = feature // lax.axis_size("rep")
    first_row = lax.axis_index("rep") * half_rows
    full_part = lax.dot_general(
        row_data, grad_low, (((0,), (0,)), ((), ())), preferred_element_type=jnp.float32
    )
    whole_w, grad_vec = lax.psum((full_part, vec_part), "rep")
    grad_w = lax.dynamic_slice_in_dim(whole_w, first_row, half_rows, 0)
    new_first_w = beta_one * first_w[0] + (1.0 - beta_one) * grad_w
    new_second_w = beta_two * second_w[0] + (1.0 - beta_two) * grad_w * grad_w
    old_rows = lax.dynamic_slice_in_dim(w_in[0], first_row, half_rows, 0).astype(jnp.float32)
    new_half = (old_rows - learn_rate * new_first_w / (jnp.sqrt(new_second_w) + epsilon)).astype(
        jnp.bfloat16
    )
    new_w_in = lax.all_gather(new_half, "rep", axis=0, tiled=True)
    vector = jnp.stack([bias_in[0], w_out[0]]).astype(jnp.float32)
    new_first_vec = beta_one * first_vec[0] + (1.0 - beta_one) * grad_vec
    new_second_vec = beta_two * second_vec[0] + (1.0 - beta_two) * grad_vec * grad_vec
    new_vec = (vector - learn_rate * new_first_vec / (jnp.sqrt(new_second_vec) + epsilon)).astype(
        jnp.bfloat16
    )
    return (
        new_w_in[None],
        new_vec[None],
        new_first_w[None],
        new_second_w[None],
        new_first_vec[None],
        new_second_vec[None],
    )


def solution(mesh):
    placed = (
        P(("dp", "head", "rep"), None, None),
        P(("dp", "head", "rep"), None),
        P(("dp", "head", "rep"), None, None),
        P(("dp", "head"), None, None),
        P(("dp", "head"), None),
        P(("dp", "head"), None),
        P(("dp", "head"), "rep", None),
        P(("dp", "head"), "rep", None),
        P(("dp", "head"), None, None),
        P(("dp", "head"), None, None),
    )
    return jax.shard_map(
        per_device,
        mesh=mesh,
        in_specs=placed,
        out_specs=(
            P(("dp", "head"), None, None),
            P(("dp", "head"), None, None),
            P(("dp", "head"), "rep", None),
            P(("dp", "head"), "rep", None),
            P(("dp", "head"), None, None),
            P(("dp", "head"), None, None),
        ),
        check_vma=False,
    )
```

profile of v0, /device:TPU:1, one launch (start us, length us, event | category | flops | bytes accessed | tf_op | source)
XLA Modules:
  0.0 236.4 jit_solution(17417560200644279252)
XLA Ops:
  7.2 0.8 copy.30
  7.9 0.1 eq.36
  8.1 0.1 fusion.10
  8.2 0.2 reduce_window_sum.11
  8.3 0.2 select_reduce_fusion
  8.5 0.7 add_convert_fusion
  9.2 0.1 copy.32
  9.3 0.2 convolution_convert_fusion.1
  9.5 0.8 copy.33
  10.3 16.3 %all-to-all-start.1 = ((bf16[128,2,8]{2,1,0:T(2,128)(2,1)}), bf16[128,2,8]{2,1,0:T(2,128)(2,1)S(1)}, u32[]{:S(2)}, u32[]{:S(2)}) async-start(bf16[128,2,8]{2,1,0:T(2,128)(2,1)} %bitcast.4), calls=%async_computation.1 | async-start | bytes 131072 | tf_op jit(solution)/shard_map/all_to_all | solution.py:43
  26.6 0.1 reduce_sum.48
  26.8 1.5 copy.34
  28.3 0.7 multiply_add_fusion
  29.1 1.4 convolution_convert_fusion
  30.5 3.1 %copy.35 = bf16[32,8,8,1152]{3,2,1,0:T(8,128)(2,1)} copy(bf16[32,8,8,1152]{3,1,2,0:T(8,128)(2,1)S(1)} %bitcast.56) | data formatting | bytes 9437184
  33.6 3.6 %all-to-all-done.1 = bf16[128,2,8]{2,1,0:T(2,128)(2,1)S(1)} async-done(((bf16[128,2,8]{2,1,0:T(2,128)(2,1)}), bf16[128,2,8]{2,1,0:T(2,128)(2,1)S(1)}, u32[]{:S(2)}, u32[]{:S(2)}) %all-to-all-start.1) | async-done | bytes 4128 | tf_op jit(solution)/shard_map/all_to_all | solution.py:43
  37.2 10.3 %all-to-all-start = ((bf16[128,2,8,1152]{3,2,1,0:T(8,128)(2,1)}), bf16[128,2,8,1152]{3,2,1,0:T(8,128)(2,1)}, u32[]{:S(2)}, u32[]{:S(2)}) async-start(bf16[128,2,8,1152]{3,2,1,0:T(8,128)(2,1)} %bitcast.55), calls=%async_computation | async-start | bytes 9437184 | tf_op jit(solution)/shard_map/all_to_all | solution.py:42
  47.5 0.2 all-reduce.2.cloned.1.call-start
  47.7 0.1 convert_compare_fusion
  47.8 0.1 gt.15
  48.0 0.2 sub.27
  48.2 103.3 %all-to-all-done = bf16[128,2,8,1152]{3,2,1,0:T(8,128)(2,1)} async-done(((bf16[128,2,8,1152]{3,2,1,0:T(8,128)(2,1)}), bf16[128,2,8,1152]{3,2,1,0:T(8,128)(2,1)}, u32[]{:S(2)}, u32[]{:S(2)}) %all-to-all-start) | async-done | bytes 4718624 | tf_op jit(solution)/shard_map/all_to_all | solution.py:42
  151.5 7.0 %multiply_reduce_fusion.1 = (f32[2048]{0:T(1024)S(1)}, f32[2048,768]{1,0:T(8,128)S(1)}) fusion(f32[768]{0:T(1024)S(1)} %get-tuple-element.16, f32[768]{0:T(1024)S(1)} %get-tuple-element.17, bf16[2048,1152]{1,0:T(8,128)(2,1)} %bitcast.2, bf16[1,1152,768]{2,1,0:T(8,128)(2,1)S(1)} %copy-done.3), kind=kOutput, calls=%fused_computation.3 | convolution fusion | flops 3634886656 | bytes 12793856 | tf_op jit(solution)/shard_map/dot_general | solution.py:51
  158.6 2.6 %copy-done = f32[2048,768]{1,0:T(8,128)} copy-done((f32[2048,768]{1,0:T(8,128)}, f32[2048,768]{1,0:T(8,128)S(1)}, u32[]{:S(2)}) %copy-start) | copy-done | bytes 6291480
  161.2 9.1 %fusion.1 = f32[1152,768]{1,0:T(8,128)} fusion(bf16[2048,1152]{1,0:T(8,128)(2,1)} %bitcast.2, f32[2048,768]{1,0:T(8,128)S(1)} %get-tuple-element.15, f32[2048]{0:T(1024)S(1)} %subtract_select_fusion, f32[768]{0:T(1024)S(1)} %get-tuple-element.16, f32[768]{0:T(1024)S(1)} %get-tuple-element.17), kind=kOutput, calls=%fused_computation.6 | convolution fusion | flops 3641180160 | bytes 14563328 | tf_op jit(solution)/shard_map/dot_general | solution.py:63
  170.4 34.5 %all-reduce.2.cloned.1.call-done = f32[1152,768]{1,0:T(8,128)} async-done(((f32[1152,768]{1,0:T(8,128)}), f32[1152,768]{1,0:T(8,128)}) %all-reduce.2.cloned.1.call-update) | async-done | bytes 3538960 | tf_op jit(solution)/shard_map/psum | solution.py:66
  204.9 4.9 %fusion.8 = (f32[1,576,768]{2,1,0:T(8,128)}, bf16[576,768]{1,0:T(8,128)(2,1)}, f32[1,576,768]{2,1,0:T(8,128)}) fusion(f32[1152,768]{1,0:T(8,128)} %all-reduce.2.cloned.1.call-done, s32[]{:T(128)S(6)} %select_n.12, f32[1,576,768]{2,1,0:T(8,128)S(1)} %copy-done.1, f32[1,576,768]{2,1,0:T(8,128)S(1)} %copy-done.2, bf16[1,1152,768]{2,1,0:T(8,128)(2,1)} %param.13), kind=kLoop, calls=%fused_computation.17 | loop fusion | flops 5750784 | bytes 10616836 | tf_op jit(solution)/shard_map/broadcast_in_dim | solution.py:85
  209.9 5.3 %fusion.16 = (f32[768]{0:T(1024)S(1)}, f32[768]{0:T(1024)S(1)}) fusion(f32[2048,768]{1,0:T(8,128)} %copy-done, f32[768]{0:T(1024)S(1)} %get-tuple-element.17, f32[768]{0:T(1024)S(1)} %get-tuple-element.16, f32[2048]{0:T(1024)S(1)} %subtract_select_fusion), kind=kLoop, calls=%fused_computation.42 | loop fusion | flops 22018560 | bytes 6311936 | tf_op jit(solution)/shard_map/reduce_sum | solution.py:60
  215.2 2.5 %psum.15 = f32[2,768]{1,0:T(2,128)S(1)} all-reduce(f32[2,768]{1,0:T(2,128)S(1)} %pad_maximum_fusion), channel_id=1, replica_groups=mesh['dp'=32,'head'=4,'rep'=2] {'rep'}, use_global_device_ids=true, to_apply=%region_7.8 | all-reduce | flops 1536 | bytes 12288 | tf_op jit(solution)/shard_map/psum | solution.py:66
  217.7 0.6 fusion.15
  218.4 8.4 %all-gather.2.cloned.1.call-done = bf16[1152,768]{1,0:T(8,128)(2,1)} async-done(((bf16[576,768]{1,0:T(8,128)(2,1)}), bf16[1152,768]{1,0:T(8,128)(2,1)}) %all-gather.2.cloned.1.call-update) | async-done | bytes 1769488 | tf_op jit(solution)/shard_map/all_gather | solution.py:74
  226.8 2.8 %copy.38 = bf16[1,1152,768]{2,1,0:T(8,128)(2,1)} copy(bf16[1,1152,768]{2,1,0:T(8,128)(2,1)} %bitcast.58) | data formatting | bytes 3538944
  (31 shorter events, 0.4 us)
Async XLA Ops:
  10.3 26.9 %all-to-all-start.1 = ((bf16[128,2,8]{2,1,0:T(2,128)(2,1)}), bf16[128,2,8]{2,1,0:T(2,128)(2,1)S(1)}, u32[]{:S(2)}, u32[]{:S(2)}) async-start(bf16[128,2,8]{2,1,0:T(2,128)(2,1)} %bitcast.4), calls=%async_computation.1 | async-start | bytes 131072 | tf_op jit(solution)/shard_map/all_to_all | solution.py:43
  37.2 10.5 %copy-start.4 = (bf16[1,768]{1,0:T(2,128)(2,1)S(1)}, bf16[1,768]{1,0:T(2,128)(2,1)}, u32[]{:S(2)}) copy-start(bf16[1,768]{1,0:T(2,128)(2,1)} %param.15) | copy-start | bytes 4612
  37.2 10.5 %copy-start.6 = (bf16[1,768]{1,0:T(2,128)(2,1)S(1)}, bf16[1,768]{1,0:T(2,128)(2,1)}, u32[]{:S(2)}) copy-start(bf16[1,768]{1,0:T(2,128)(2,1)} %param.14) | copy-start | bytes 4612
  37.2 114.4 %copy-start.3 = (bf16[1,1152,768]{2,1,0:T(8,128)(2,1)S(1)}, bf16[1,1152,768]{2,1,0:T(8,128)(2,1)}, u32[]{:S(2)}) copy-start(bf16[1,1152,768]{2,1,0:T(8,128)(2,1)} %param.13) | copy-start | bytes 5308420
  37.2 114.4 %all-to-all-start = ((bf16[128,2,8,1152]{3,2,1,0:T(8,128)(2,1)}), bf16[128,2,8,1152]{3,2,1,0:T(8,128)(2,1)}, u32[]{:S(2)}, u32[]{:S(2)}) async-start(bf16[128,2,8,1152]{3,2,1,0:T(8,128)(2,1)} %bitcast.55), calls=%async_computation | async-start | bytes 9437184 | tf_op jit(solution)/shard_map/all_to_all | solution.py:42
  47.5 157.4 %all-reduce.2.cloned.1.call-start = ((), (), s32[]{:S(2)}) async-start(), calls=%async_computation.2 | async-start | bytes 7077888 | tf_op jit(solution)/shard_map/psum | solution.py:66
  158.5 2.7 %copy-start = (f32[2048,768]{1,0:T(8,128)}, f32[2048,768]{1,0:T(8,128)S(1)}, u32[]{:S(2)}) copy-start(f32[2048,768]{1,0:T(8,128)S(1)} %get-tuple-element.15) | copy-start | bytes 18874372
  170.3 34.6 %copy-start.1 = (f32[1,576,768]{2,1,0:T(8,128)S(1)}, f32[1,576,768]{2,1,0:T(8,128)}, u32[]{:S(2)}) copy-start(f32[1,576,768]{2,1,0:T(8,128)} %param.17) | copy-start | bytes 5308420
  170.3 34.6 %copy-start.2 = (f32[1,576,768]{2,1,0:T(8,128)S(1)}, f32[1,576,768]{2,1,0:T(8,128)}, u32[]{:S(2)}) copy-start(f32[1,576,768]{2,1,0:T(8,128)} %param.16) | copy-start | bytes 5308420
  170.3 56.5 %all-gather.2.cloned.1.call-start = ((), (), s32[]{:S(2)}) async-start(), calls=%async_computation.3 | async-start | bytes 2654208 | tf_op jit(solution)/shard_map/all_gather | solution.py:74
  209.9 7.9 %copy-start.5 = (bf16[1,768]{1,0:T(2,128)(2,1)S(1)}, bf16[1,768]{1,0:T(2,128)(2,1)}, u32[]{:S(2)}) copy-start(bf16[1,768]{1,0:T(2,128)(2,1)} %param.15) | copy-start | bytes 4612
  209.9 7.9 %copy-start.7 = (bf16[1,768]{1,0:T(2,128)(2,1)S(1)}, bf16[1,768]{1,0:T(2,128)(2,1)}, u32[]{:S(2)}) copy-start(bf16[1,768]{1,0:T(2,128)(2,1)} %param.14) | copy-start | bytes 4612
  209.9 7.9 %copy-start.8 = (f32[1,2,768]{2,1,0:T(2,128)S(1)}, f32[1,2,768]{2,1,0:T(2,128)}, u32[]{:S(2)}) copy-start(f32[1,2,768]{2,1,0:T(2,128)} %param.19) | copy-start | bytes 18436
  209.9 7.9 %copy-start.9 = (f32[1,2,768]{2,1,0:T(2,128)S(1)}, f32[1,2,768]{2,1,0:T(2,128)}, u32[]{:S(2)}) copy-start(f32[1,2,768]{2,1,0:T(2,128)} %param.18) | copy-start | bytes 18436
Sparse Core Ops, SparseCore 0:
  170.4 34.4 all-reduce.1
  210.0 16.7 all-gather.1
where the time goes:
time: 237 us; the launch traced here: 236 us
  waiting for transfers between devices  150 us (63%)
  starting transfers between devices  26.9 us (11%)
  matrix products  17.7 us (7%)
  between operations  14.3 us (6%)
  other arithmetic  13 us (5%)
  local copies, waits for them, and re-layouts  12.3 us (5%)
  blocking collectives  2.51 us (1%)
    all_to_all x1, waiting for transfers between devices, per_device(): lax.all_to_all(direct_rows, ('dp', 'head'), split_axis=0, concat_axis=0,...  103 us
    psum x1, waiting for transfers between devices, per_device(): whole_w, grad_vec = lax.psum((full_part, vec_part), 'rep')  34.5 us
    all_to_all x1, starting transfers between devices, per_device(): lax.all_to_all(direct_marks, ('dp', 'head'), split_axis=0, concat_axis=0,...  16.3 us
    unnamed x24, local copies, waits for them, and re-layouts  10.8 us
    all_to_all x1, starting transfers between devices, per_device(): lax.all_to_all(direct_rows, ('dp', 'head'), split_axis=0, concat_axis=0,...  10.3 us
    dot_general x1, matrix products, per_device(): lax.dot_general(row_data, grad_low, (((0,), (0,)), ((), ())), preferred_e...  9.07 us
    all_gather x1, waiting for transfers between devices, per_device(): new_w_in = lax.all_gather(new_half, 'rep', axis=0, tiled=True)  8.39 us
    dot_general x1, matrix products, per_device(): jnp.dot(row_data, w_in[0], preferred_element_type=jnp.float32)  7 us
  transfers between devices with their start and end apart: 4, of which 4 were waited for; matrix products, arithmetic and copies ran while one was open for 6% of the time, Pallas kernels for 0%

commit v1 on v0

--- a/solution.py
+++ b/solution.py
@@ -71,7 +71,9 @@
     new_half = (old_rows - learn_rate * new_first_w / (jnp.sqrt(new_second_w) + epsilon)).astype(
         jnp.bfloat16
     )
-    new_w_in = lax.all_gather(new_half, "rep", axis=0, tiled=True)
+    new_w_in = jnp.concatenate(
+        lax.all_to_all(jnp.stack([new_half] * lax.axis_size("rep")), "rep", 0, 0), axis=0
+    )
     vector = jnp.stack([bias_in[0], w_out[0]]).astype(jnp.float32)
     new_first_vec = beta_one * first_vec[0] + (1.0 - beta_one) * grad_vec
     new_second_vec = beta_two * second_vec[0] + (1.0 - beta_two) * grad_vec * grad_vec

time: 237 us -> 223 us (0.941)
  waiting for transfers between devices: 150 us -> 128 us
  blocking collectives: 2.51 us -> 11.7 us
    psum x1, waiting for transfers between devices: 34.5 us -> 21 us  [per_device(): whole_w, grad_vec = lax.psum((full_part, vec_part), 'rep')]
    all_gather x1 -> x0, waiting for transfers between devices: 8.39 us -> none  [per_device(): new_w_in = lax.all_gather(new_half, 'rep', axis=0, tiled=True)]
    all_to_all x0 -> x1, blocking collectives: none -> 5.01 us  [per_device(): lax.all_to_all(jnp.stack([new_half] * lax.axis_size('rep')), 'rep', 0, 0)]
    psum x1, blocking collectives: 2.51 us -> 6.74 us  [per_device(): whole_w, grad_vec = lax.psum((full_part, vec_part), 'rep')]
    unnamed x24 -> x16, local copies, waits for them, and re-layouts: 10.8 us -> 9.15 us
  transfers between devices with their start and end apart: 4 -> 3, of which waited for: 4 -> 3; matrix products, arithmetic and copies ran while one was open for 6% -> 6% of each run, Pallas kernels for 0% -> 0%
where the time goes in v1:
time: 223 us
  waiting for transfers between devices  128 us (57%)
  starting transfers between devices  26.8 us (12%)
  matrix products  17.7 us (8%)
  between operations  14.2 us (6%)
  other arithmetic  13.7 us (6%)
  blocking collectives  11.7 us (5%)
  local copies, waits for them, and re-layouts  10.7 us (5%)
    all_to_all x1, waiting for transfers between devices, per_device(): lax.all_to_all(direct_rows, ('dp', 'head'), split_axis=0, concat_axis=0,...  103 us
    psum x1, waiting for transfers between devices, per_device(): whole_w, grad_vec = lax.psum((full_part, vec_part), 'rep')  21 us
    all_to_all x1, starting transfers between devices, per_device(): lax.all_to_all(direct_marks, ('dp', 'head'), split_axis=0, concat_axis=0,...  16.3 us
    all_to_all x1, starting transfers between devices, per_device(): lax.all_to_all(direct_rows, ('dp', 'head'), split_axis=0, concat_axis=0,...  10.3 us
    unnamed x16, local copies, waits for them, and re-layouts  9.15 us
    dot_general x1, matrix products, per_device(): lax.dot_general(row_data, grad_low, (((0,), (0,)), ((), ())), preferred_e...  9.07 us
    dot_general x1, matrix products, per_device(): jnp.dot(row_data, w_in[0], preferred_element_type=jnp.float32)  7 us
    psum x1, blocking collectives, per_device(): whole_w, grad_vec = lax.psum((full_part, vec_part), 'rep')  6.74 us
  transfers between devices with their start and end apart: 3, of which 3 were waited for; matrix products, arithmetic and copies ran while one was open for 6% of the time, Pallas kernels for 0%

profile of v1, /device:TPU:1, one launch (start us, length us, event | category | flops | bytes accessed | tf_op | source)
XLA Modules:
  0.0 222.8 jit_solution(6301524641128057739)
XLA Ops:
  7.2 0.8 copy.30
  7.9 0.1 eq.36
  8.2 0.2 reduce_window_sum.11
  8.3 0.2 select_reduce_fusion
  8.5 0.7 add_convert_fusion
  9.2 0.1 copy.32
  9.3 0.2 convolution_convert_fusion.1
  9.5 0.8 copy.33
  10.3 16.3 %all-to-all-start.1 = ((bf16[128,2,8]{2,1,0:T(2,128)(2,1)}), bf16[128,2,8]{2,1,0:T(2,128)(2,1)S(1)}, u32[]{:S(2)}, u32[]{:S(2)}) async-start(bf16[128,2,8]{2,1,0:T(2,128)(2,1)} %bitcast.4), calls=%async_computation.1 | async-start | bytes 131072 | tf_op jit(solution)/shard_map/all_to_all | solution.py:43
  26.6 0.1 reduce_sum.48
  26.8 1.5 copy.34
  28.3 0.7 multiply_add_fusion
  29.1 1.4 convolution_convert_fusion
  30.5 3.1 %copy.35 = bf16[32,8,8,1152]{3,2,1,0:T(8,128)(2,1)} copy(bf16[32,8,8,1152]{3,1,2,0:T(8,128)(2,1)S(1)} %bitcast.60) | data formatting | bytes 9437184
  33.6 3.6 %all-to-all-done.1 = bf16[128,2,8]{2,1,0:T(2,128)(2,1)S(1)} async-done(((bf16[128,2,8]{2,1,0:T(2,128)(2,1)}), bf16[128,2,8]{2,1,0:T(2,128)(2,1)S(1)}, u32[]{:S(2)}, u32[]{:S(2)}) %all-to-all-start.1) | async-done | bytes 4128 | tf_op jit(solution)/shard_map/all_to_all | solution.py:43
  37.2 10.3 %all-to-all-start = ((bf16[128,2,8,1152]{3,2,1,0:T(8,128)(2,1)}), bf16[128,2,8,1152]{3,2,1,0:T(8,128)(2,1)}, u32[]{:S(2)}, u32[]{:S(2)}) async-start(bf16[128,2,8,1152]{3,2,1,0:T(8,128)(2,1)} %bitcast.59), calls=%async_computation | async-start | bytes 9437184 | tf_op jit(solution)/shard_map/all_to_all | solution.py:42
  47.5 0.2 all-reduce.2.cloned.1.call-start
  47.7 0.1 convert_compare_fusion
  47.8 0.1 gt.15
  48.0 0.2 sub.27
  48.2 103.3 %all-to-all-done = bf16[128,2,8,1152]{3,2,1,0:T(8,128)(2,1)} async-done(((bf16[128,2,8,1152]{3,2,1,0:T(8,128)(2,1)}), bf16[128,2,8,1152]{3,2,1,0:T(8,128)(2,1)}, u32[]{:S(2)}, u32[]{:S(2)}) %all-to-all-start) | async-done | bytes 4718624 | tf_op jit(solution)/shard_map/all_to_all | solution.py:42
  151.5 7.0 %multiply_reduce_fusion.1 = (f32[2048]{0:T(1024)S(1)}, f32[2048,768]{1,0:T(8,128)S(1)}) fusion(f32[768]{0:T(1024)S(1)} %get-tuple-element.16, f32[768]{0:T(1024)S(1)} %get-tuple-element.17, bf16[2048,1152]{1,0:T(8,128)(2,1)} %bitcast.2, bf16[1,1152,768]{2,1,0:T(8,128)(2,1)S(1)} %copy-done.3), kind=kOutput, calls=%fused_computation.3 | convolution fusion | flops 3634886656 | bytes 12793856 | tf_op jit(solution)/shard_map/dot_general | solution.py:51
  158.6 2.6 %copy-done = f32[2048,768]{1,0:T(8,128)} copy-done((f32[2048,768]{1,0:T(8,128)}, f32[2048,768]{1,0:T(8,128)S(1)}, u32[]{:S(2)}) %copy-start) | copy-done | bytes 6291480
  161.2 9.1 %fusion.1 = f32[1152,768]{1,0:T(8,128)} fusion(bf16[2048,1152]{1,0:T(8,128)(2,1)} %bitcast.2, f32[2048,768]{1,0:T(8,128)S(1)} %get-tuple-element.15, f32[2048]{0:T(1024)S(1)} %subtract_select_fusion, f32[768]{0:T(1024)S(1)} %get-tuple-element.16, f32[768]{0:T(1024)S(1)} %get-tuple-element.17), kind=kOutput, calls=%fused_computation.6 | convolution fusion | flops 3641180160 | bytes 14563328 | tf_op jit(solution)/shard_map/dot_general | solution.py:63
  170.3 5.4 %fusion.17 = (f32[768]{0:T(1024)S(1)}, f32[768]{0:T(1024)S(1)}) fusion(f32[2048,768]{1,0:T(8,128)} %copy-done, f32[768]{0:T(1024)S(1)} %get-tuple-element.17, f32[768]{0:T(1024)S(1)} %get-tuple-element.16, f32[2048]{0:T(1024)S(1)} %subtract_select_fusion), kind=kLoop, calls=%fused_computation.44 | loop fusion | flops 22018560 | bytes 6311936 | tf_op jit(solution)/shard_map/reduce_sum | solution.py:60
  175.8 6.7 %psum.15 = f32[2,768]{1,0:T(2,128)S(1)} all-reduce(f32[2,768]{1,0:T(2,128)S(1)} %pad_maximum_fusion.1), channel_id=1, replica_groups=mesh['dp'=32,'head'=4,'rep'=2] {'rep'}, use_global_device_ids=true, to_apply=%region_7.8 | all-reduce | flops 1536 | bytes 12288 | tf_op jit(solution)/shard_map/psum | solution.py:66
  182.5 1.4 fusion.16
  183.9 21.0 %all-reduce.2.cloned.1.call-done = f32[1152,768]{1,0:T(8,128)} async-done(((f32[1152,768]{1,0:T(8,128)}), f32[1152,768]{1,0:T(8,128)}) %all-reduce.2.cloned.1.call-update) | async-done | bytes 3538960 | tf_op jit(solution)/shard_map/psum | solution.py:66
  204.9 4.7 %fusion.9 = (f32[1,576,768]{2,1,0:T(8,128)}, bf16[1,576,768]{2,1,0:T(8,128)(2,1)S(1)}, f32[1,576,768]{2,1,0:T(8,128)}) fusion(f32[1152,768]{1,0:T(8,128)} %all-reduce.2.cloned.1.call-done, s32[]{:T(128)S(6)} %select_n.12, f32[1,576,768]{2,1,0:T(8,128)S(1)} %copy-done.1, f32[1,576,768]{2,1,0:T(8,128)S(1)} %copy-done.2, bf16[1,1152,768]{2,1,0:T(8,128)(2,1)} %param.13), kind=kLoop, calls=%fused_computation.19 | loop fusion | flops 5750784 | bytes 10616836 | tf_op jit(solution)/shard_map/broadcast_in_dim | solution.py:87
  209.6 0.2 pad_maximum_fusion
  209.7 5.0 %all_to_all.15 = bf16[2,576,768]{2,1,0:T(8,128)(2,1)S(1)} all-to-all(bf16[2,576,768]{2,1,0:T(8,128)(2,1)S(1)} %pad_maximum_fusion), channel_id=1, replica_groups=mesh['dp'=32,'head'=4,'rep'=2] {'rep'}, dimensions={0} | all-to-all | bytes 3538944 | tf_op jit(solution)/shard_map/all_to_all | solution.py:75
  214.7 1.2 copy.38
  (22 shorter events, 0.4 us)
Async XLA Ops:
  10.3 26.9 %all-to-all-start.1 = ((bf16[128,2,8]{2,1,0:T(2,128)(2,1)}), bf16[128,2,8]{2,1,0:T(2,128)(2,1)S(1)}, u32[]{:S(2)}, u32[]{:S(2)}) async-start(bf16[128,2,8]{2,1,0:T(2,128)(2,1)} %bitcast.4), calls=%async_computation.1 | async-start | bytes 131072 | tf_op jit(solution)/shard_map/all_to_all | solution.py:43
  37.2 10.5 %copy-start.4 = (bf16[1,768]{1,0:T(2,128)(2,1)S(1)}, bf16[1,768]{1,0:T(2,128)(2,1)}, u32[]{:S(2)}) copy-start(bf16[1,768]{1,0:T(2,128)(2,1)} %param.15) | copy-start | bytes 4612
  37.2 10.5 %copy-start.5 = (bf16[1,768]{1,0:T(2,128)(2,1)S(1)}, bf16[1,768]{1,0:T(2,128)(2,1)}, u32[]{:S(2)}) copy-start(bf16[1,768]{1,0:T(2,128)(2,1)} %param.14) | copy-start | bytes 4612
  37.2 114.4 %copy-start.3 = (bf16[1,1152,768]{2,1,0:T(8,128)(2,1)S(1)}, bf16[1,1152,768]{2,1,0:T(8,128)(2,1)}, u32[]{:S(2)}) copy-start(bf16[1,1152,768]{2,1,0:T(8,128)(2,1)} %param.13) | copy-start | bytes 5308420
  37.2 114.4 %all-to-all-start = ((bf16[128,2,8,1152]{3,2,1,0:T(8,128)(2,1)}), bf16[128,2,8,1152]{3,2,1,0:T(8,128)(2,1)}, u32[]{:S(2)}, u32[]{:S(2)}) async-start(bf16[128,2,8,1152]{3,2,1,0:T(8,128)(2,1)} %bitcast.59), calls=%async_computation | async-start | bytes 9437184 | tf_op jit(solution)/shard_map/all_to_all | solution.py:42
  47.5 157.4 %all-reduce.2.cloned.1.call-start = ((), (), s32[]{:S(2)}) async-start(), calls=%async_computation.3 | async-start | bytes 7077888 | tf_op jit(solution)/shard_map/psum | solution.py:66
  158.5 2.7 %copy-start = (f32[2048,768]{1,0:T(8,128)}, f32[2048,768]{1,0:T(8,128)S(1)}, u32[]{:S(2)}) copy-start(f32[2048,768]{1,0:T(8,128)S(1)} %get-tuple-element.15) | copy-start | bytes 18874372
  170.3 34.6 %copy-start.1 = (f32[1,576,768]{2,1,0:T(8,128)S(1)}, f32[1,576,768]{2,1,0:T(8,128)}, u32[]{:S(2)}) copy-start(f32[1,576,768]{2,1,0:T(8,128)} %param.17) | copy-start | bytes 5308420
  170.3 34.6 %copy-start.2 = (f32[1,576,768]{2,1,0:T(8,128)S(1)}, f32[1,576,768]{2,1,0:T(8,128)}, u32[]{:S(2)}) copy-start(f32[1,576,768]{2,1,0:T(8,128)} %param.16) | copy-start | bytes 5308420
Sparse Core Ops, SparseCore 0:
  170.4 34.4 all-reduce.1
